TPU v7x, 32 devices: a whole 2x2x4 slice. The times are simulated.
32 devices in a mesh: sec: 4 (over x, core), lat: 2 (over y), col: 4 (over z).
Axes of the slice: x: 2, y: 2, z: 4, core: 2. Of those that a mesh axis runs over, the one named last changes fastest.
Arguments:
- state: float32 [1, 4, 28, 192, 384], P(None, 'sec', None, 'lat', 'col'), may hold values from -6 to 6
- forcing: float32 [1, 4, 28, 192, 384], P(None, 'sec', None, 'lat', 'col'), may hold values from -4 to 4
- crm_moisture: bfloat16 [1, 32, 28, 8, 4, 2304], P(None, None, None, ('sec', 'lat'), 'col'), may hold values from -6 to 6
- cloud_order: int32 [4, 2, 9216], P('col', 'lat'), may hold values from 0 to 9215, each once within a row
- wave_table: int32 [128], replicated, may hold values from 0 to 127, each once
Outputs:
- state_out: float32 [1, 4, 28, 192, 384], P(None, 'sec', None, 'lat', 'col')
- spectral: float32 [4, 1, 28, 128, 2, 128], P('sec', None, 'col', 'lat')
Inputs may be any that keep to these rules, and one draw needn't show every extreme that they name: `cloud_order`: every row lists each of the 9216 columns of a band block once. `wave_table`: each wavenumber stands in exactly one slot.
All inputs are finite; a program needn't handle non-finite values.
Results may differ from a plain program's by a relative error of at most 0.0003.
Values sent between devices are 32-bit elements; how exact they have to be, the bound alone decides.
A program may use at most 128 MiB of HBM per device.

v0:
```python
import math
import jax
import jax.numpy as jnp
from jax import lax
from jax.sharding import PartitionSpec as P

NLON = 384
NLAT = 192
MMAX = 128
NSUB = 4
COURANT_SCALE = 0.4
CONDENSE = 0.5


def transport(values, courant, mixing):
    forward = jnp.roll(values, -1, axis=0)
    behind = jnp.roll(values, 1, axis=0)
    return -0.5 * courant * (forward - behind) + mixing * (forward - 2.0 * values + behind)


def cloud_model(vertical_state_stack, forcing, vapour_mass_fraction):
    wind_u = vertical_state_stack[0]
    wind_v = vertical_state_stack[1]
    atmospheric_warmth = vertical_state_stack[2]
    humidity = vertical_state_stack[3]
    courant = COURANT_SCALE * jnp.tanh(wind_u)
    mixing = 0.2 + 0.5 * jnp.abs(courant)
    convective_warming_rate = jnp.broadcast_to(atmospheric_warmth, vapour_mass_fraction.shape)
    crm_water = humidity + vapour_mass_fraction
    start_water = crm_water
    ground_precipitation = jnp.zeros_like(atmospheric_warmth)
    for substep in range(NSUB):
        heat_move = transport(convective_warming_rate, courant, mixing)
        water_move = transport(crm_water, courant, mixing)
        condensed = CONDENSE * jnp.maximum(crm_water - convective_warming_rate, 0.0)
        convective_warming_rate = (
            convective_warming_rate + heat_move + condensed + forcing[2] / NSUB
        )
        crm_water = crm_water + water_move - condensed + forcing[3] / NSUB
        ground_precipitation = ground_precipitation + jnp.mean(condensed, axis=0)
    ground_precipitation = ground_precipitation / NSUB
    zonal_velocity_rate = -ground_precipitation * wind_u + forcing[0]
    meridional_velocity_rate = -ground_precipitation * wind_v + forcing[1]
    warming_rate_change = jnp.mean(convective_warming_rate, axis=0) - atmospheric_warmth
    vapour_rate_change = jnp.mean(crm_water - start_water, axis=0)
    return jnp.stack(
        (zonal_velocity_rate, meridional_velocity_rate, warming_rate_change, vapour_rate_change)
    )


def trig_table(longitudes, wave_numbers):
    phase = (longitudes[:, None] * wave_numbers[None, :] % NLON).astype(jnp.float32) * (
        2.0 * math.pi / NLON
    )
    return jnp.stack((jnp.cos(phase), jnp.sin(phase)), axis=1) / math.sqrt(NLON)


def legendre_table(orders):
    colatitude = (jnp.arange(NLAT, dtype=jnp.int32).astype(jnp.float32) + 0.5) * (math.pi / NLAT)
    cosine = jnp.cos(colatitude)[None, :]
    sine_lat = jnp.sin(colatitude)
    order_col = orders.astype(jnp.float32)[:, None]
    log_diag = 0.5 * (
        lax.lgamma(order_col + 1.5) - lax.lgamma(jnp.float32(1.5)) - lax.lgamma(order_col + 1.0)
    )
    log_diag = log_diag + order_col * jnp.log(sine_lat)[None, :] - 0.5 * math.log(2.0)
    diagonal = jnp.exp(log_diag)
    empty = jnp.zeros_like(diagonal)

    def march_forward(carried, degree):
        previous, current = carried
        deg_float = degree.astype(jnp.float32)
        active = deg_float > order_col
        numerator = jnp.where(active, 4.0 * deg_float * deg_float - 1.0, 1.0)
        bottom = jnp.where(active, deg_float * deg_float - order_col * order_col, 1.0)
        lower_deg = deg_float - 1.0
        retreat = jnp.sqrt(
            jnp.maximum(lower_deg * lower_deg - order_col * order_col, 0.0)
            / (4.0 * lower_deg * lower_deg - 1.0)
        )
        grown = jnp.sqrt(numerator / bottom) * (cosine * current - retreat * previous)
        fresh_row = jnp.where(active, grown, jnp.where(deg_float == order_col, diagonal, 0.0))
        return ((current, fresh_row), fresh_row)

    _, legendre_rows = lax.scan(
        march_forward, (empty, empty), jnp.arange(MMAX, dtype=jnp.int32), unroll=8
    )
    weights = sine_lat / math.sqrt(NLAT)
    return legendre_rows * weights[None, None, :]


def shards(state, forcing, crm_moisture, cloud_order, wave_table):
    members, _, levels, band_rows, lon_block = state.shape
    sections = lax.axis_size("sec")
    lat_bands = lax.axis_size("lat")
    block_cols = band_rows * lon_block
    targets = sections * lat_bands
    per_target = block_cols // targets
    run_cols = lat_bands * per_target
    slot_list = cloud_order[0, 0]
    flat_state = state[:, 0].reshape(members, levels, block_cols)
    flat_force = forcing[:, 0].reshape(members, levels, block_cols)
    stacked = jnp.stack((flat_state, flat_force))
    use_matrix = block_cols <= 2048
    if use_matrix:
        column_ids = jnp.arange(block_cols, dtype=jnp.int32)
        selector = (slot_list[:, None] == column_ids[None, :]).astype(jnp.float32)
        selector = selector.reshape(targets, per_target, block_cols)
        by_target = jnp.einsum(
            "xelc,tpc->txelp", stacked, selector, precision=lax.Precision.HIGHEST
        )
    else:
        slot_table = slot_list.reshape(targets, per_target)
        by_target = jnp.take(stacked, slot_table, axis=3).transpose(3, 0, 1, 2, 4)
    send_width = 2 * members * levels * per_target
    outgoing = by_target.reshape(targets, 1, send_width)
    arrived = lax.all_to_all(outgoing, ("sec", "lat"), split_axis=0, concat_axis=1, tiled=True)
    arrived = arrived.reshape(sections, lat_bands, 2, members, levels, per_target)
    arrived = arrived.transpose(2, 3, 0, 4, 1, 5).reshape(2, members, sections, levels, run_cols)
    vapour_mass_fraction = crm_moisture[:, :, :, 0, 0, :].astype(jnp.float32)
    tendency = jax.vmap(cloud_model)(arrived[0], arrived[1], vapour_mass_fraction)
    back_width = members * levels * per_target
    parted = tendency.reshape(members, sections, levels, lat_bands, per_target).transpose(
        1, 3, 0, 2, 4
    )
    homeward = parted.reshape(targets, 1, back_width)
    returned = lax.all_to_all(homeward, ("sec", "lat"), split_axis=0, concat_axis=1, tiled=True)
    returned = returned.reshape(targets, members, levels, per_target)
    if use_matrix:
        column_tend = jnp.einsum(
            "telp,tpc->elc", returned, selector, precision=lax.Precision.HIGHEST
        )
    else:
        in_slot_order = returned.transpose(1, 2, 0, 3).reshape(members, levels, block_cols)
        inverse = (
            jnp.zeros((block_cols,), jnp.int32)
            .at[slot_list]
            .set(jnp.arange(block_cols, dtype=jnp.int32))
        )
        column_tend = jnp.take(in_slot_order, inverse, axis=2)
    new_state = state + column_tend.reshape(members, 1, levels, band_rows, lon_block)
    fields_now = new_state[:, 0]
    regrouped = lax.all_to_all(fields_now, "col", split_axis=1, concat_axis=3, tiled=True)
    trig_rows = trig_table(jnp.arange(NLON, dtype=jnp.int32), wave_table)
    spectra = jnp.einsum("elay,ycs->leacs", regrouped, trig_rows, precision=lax.Precision.HIGHEST)
    owner_count = MMAX // lat_bands
    owned_waves = lax.dynamic_slice_in_dim(
        wave_table, lax.axis_index("lat") * owner_count, owner_count
    )
    weighted = legendre_table(owned_waves)
    coeffs = jnp.einsum(
        "leacs,nsa->lescn",
        lax.all_to_all(spectra, "lat", split_axis=4, concat_axis=2, tiled=True),
        weighted,
        precision=lax.Precision.HIGHEST,
    )
    return (new_state, coeffs.transpose(1, 0, 2, 3, 4)[None])


def solution(mesh):
    placed = (
        P(None, "sec", None, "lat", "col"),
        P(None, "sec", None, "lat", "col"),
        P(None, None, None, ("sec", "lat"), "col", None),
        P("col", "lat", None),
        P(),
    )
    return jax.shard_map(
        shards,
        mesh=mesh,
        in_specs=placed,
        out_specs=(P(None, "sec", None, "lat", "col"), P("sec", None, "col", "lat", None, None)),
        check_vma=False,
    )
```

profile of v0, /device:TPU:0, one launch (start us, length us, event | category | flops | bytes accessed | tf_op | source)
XLA Modules:
  0.0 617.8 jit_solution(15308398719967561475)
XLA Ops:
  8.7 13.0 %maximum_bitcast_fusion = f32[2,28,9216]{1,0,2:T(2,128)} fusion(f32[1,1,28,9216]{2,0,3,1:T(1,128)} %bitcast.285, f32[1,1,28,9216]{2,0,3,1:T(1,128)} %bitcast.284), kind=kLoop, calls=%fused_computation.84 | loop fusion | flops 516096 | bytes 4128768 | tf_op jit(solution)/shard_map/stack | solution.py:103
  21.7 66.6 %gather_fusion = f32[9216,2,28]{2,1,0:T(2,128)} fusion(f32[2,28,9216]{1,0,2:T(2,128)} %maximum_bitcast_fusion, s32[9216]{0:T(1024)S(1)} %broadcast_clamp_fusion), kind=kCustom, calls=%fused_computation | custom fusion | bytes 4165632 | tf_op jit(solution)/shard_map/jit(_take)/gather | solution.py:114
  88.3 8.0 %copy.118 = f32[8,1152,2,28]{1,0,2,3:T(8,128)S(1)} copy(f32[8,1152,2,28]{3,2,1,0:T(2,128)} %bitcast.286) | data formatting | bytes 4128768 | tf_op jit(solution)/shard_map/jit(_take)/gather | solution.py:114
  100.1 30.3 %all_to_all.48 = f32[8,1,64512]{2,1,0:T(1,128)S(1)} all-to-all(f32[8,1,64512]{2,1,0:T(1,128)S(1)} %copy.96), channel_id=1, replica_groups=mesh['sec'=4,'lat'=2,'col'=4] {'sec','lat'}, dimensions={0} | all-to-all | bytes 4128768 | tf_op jit(solution)/shard_map/all_to_all | solution.py:117
  130.4 6.9 %reduce.8 = f32[8,64512]{1,0:T(8,128)} reduce(f32[8,1,64512]{2,1,0:T(1,128)S(1)} %all_to_all.48, f32[]{:T(128)} %constant.239), dimensions={1}, to_apply=%all_to_all.16.reduce_sub_computation | reduce | bytes 4128772 | tf_op jit(solution)/shard_map/all_to_all | solution.py:117
  151.4 8.7 %fusion.44 = (f32[1,32,28,2304]{3,1,2,0:T(8,128)}, f32[1,32,28,2304]{3,1,2,0:T(8,128)S(1)}) fusion(f32[1,1,28,2304]{3,1,2,0:T(1,128)S(1)} %get-tuple-element.412, f32[1,31,28,2304]{3,1,2,0:T(8,128)S(1)} %slice.206, bf16[1,32,28,1,1,2304]{5,1,4,3,2,0:T(8,128)(2,1)S(1)} %copy-done.2, f32[28,2304]{1,0:T(8,128)S(1)} %get-tuple-element.418, ...), kind=kLoop, calls=%fused_computation.94 | loop fusion | flops 33030144 | bytes 30449664 | tf_op jit(solution)/shard_map/vmap()/add | solution.py:37
  160.0 6.5 %fusion.107 = (f32[1,31,28,2304]{3,1,2,0:T(8,128)}, f32[1,31,28,2304]{3,1,2,0:T(8,128)}) fusion(f32[1,32,28,2304]{3,1,2,0:T(8,128)S(1)} %get-tuple-element.407), kind=kLoop, calls=%fused_computation.237 | loop fusion | bytes 31997952 | tf_op jit(solution)/shard_map/vmap(jit(_roll_static))/slice | solution.py:16
  166.9 15.7 %fusion.51 = (f32[28,2304]{1,0:T(8,128)}, f32[28,2304]{1,0:T(8,128)}, f32[1,32,28,2304]{3,1,2,0:T(8,128)S(1)}) fusion(f32[28,2304]{1,0:T(8,128)S(1)} %get-tuple-element.418, bf16[1,32,28,1,1,2304]{5,1,4,3,2,0:T(8,128)(2,1)S(1)} %copy-done.2, f32[28,2304]{1,0:T(8,128)S(1)} %get-tuple-element.423, f32[28,2304]{1,0:T(8,128)S(1)} %copy-done.8, ...), kind=kLoop, calls=%fused_computation.125 | loop fusion | flops 67995648 | bytes 39481344 | tf_op jit(solution)/shard_map/vmap()/reduce_sum | solution.py:40
  182.5 8.4 %fusion.105 = (f32[1,31,28,2304]{3,1,2,0:T(8,128)}, f32[1,31,28,2304]{3,1,2,0:T(8,128)}) fusion(f32[1,32,28,2304]{3,1,2,0:T(8,128)S(1)} %get-tuple-element.336), kind=kLoop, calls=%fused_computation.235 | loop fusion | bytes 31997952 | tf_op jit(solution)/shard_map/vmap(jit(_roll_static))/slice | solution.py:16
  194.3 6.4 %fusion.103 = (f32[1,31,28,2304]{3,1,2,0:T(8,128)}, f32[1,31,28,2304]{3,1,2,0:T(8,128)}) fusion(f32[1,32,28,2304]{3,1,2,0:T(8,128)S(1)} %bitcast.282), kind=kLoop, calls=%fused_computation.233 | loop fusion | bytes 31997952 | tf_op jit(solution)/shard_map/vmap(jit(_roll_static))/slice | solution.py:16
  201.9 31.2 %fusion.52 = (f32[28,2304]{1,0:T(8,128)}, f32[1,32,28,2304]{3,1,2,0:T(8,128)}, f32[1,32,28,2304]{3,1,2,0:T(8,128)}) fusion(f32[28,2304]{1,0:T(8,128)S(1)} %get-tuple-element.419, f32[1,32,28,2304]{3,1,2,0:T(8,128)} %copy-done, f32[28,2304]{1,0:T(8,128)S(1)} %get-tuple-element.418, bf16[1,32,28,1,1,2304]{5,1,4,3,2,0:T(8,128)(2,1)S(1)} %copy-done.2, ...), kind=kLoop, calls=%fused_computation.126 | loop fusion | flops 96961536 | bytes 72253440 | tf_op jit(solution)/shard_map/vmap()/reduce_sum | solution.py:40
  233.0 12.5 %fusion.97 = (f32[1,31,28,2304]{3,1,2,0:T(8,128)}, f32[1,31,28,2304]{3,1,2,0:T(8,128)}) fusion(f32[1,32,28,2304]{3,1,2,0:T(8,128)} %get-tuple-element.338), kind=kLoop, calls=%fused_computation.227 | loop fusion | bytes 31997952 | tf_op jit(solution)/shard_map/vmap(jit(_roll_static))/slice | solution.py:16
  248.9 6.4 %fusion.101 = (f32[1,31,28,2304]{3,1,2,0:T(8,128)}, f32[1,31,28,2304]{3,1,2,0:T(8,128)}) fusion(f32[1,32,28,2304]{3,1,2,0:T(8,128)S(1)} %bitcast.280), kind=kLoop, calls=%fused_computation.231 | loop fusion | bytes 31997952 | tf_op jit(solution)/shard_map/vmap(jit(_roll_static))/slice | solution.py:16
  256.4 18.1 %subtract_add_fusion = (f32[1,32,28,2304]{3,1,2,0:T(8,128)S(1)}, f32[1,32,28,2304]{3,1,2,0:T(8,128)S(1)}) fusion(f32[1,32,28,2304]{3,1,2,0:T(8,128)} %get-tuple-element.338, f32[1,31,28,2304]{3,1,2,0:T(8,128)} %get-tuple-element.383, f32[1,1,28,2304]{3,1,2,0:T(1,128)} %get-tuple-element.385, f32[1,1,28,2304]{3,1,2,0:T(1,128)} %get-tuple-element.384, ...), kind=kLoop, calls=%fused_computation.114 | loop fusion | flops 55738368 | bytes 67092480 | tf_op jit(solution)/shard_map/vmap()/add | solution.py:39
  274.5 6.4 %fusion.95 = (f32[1,31,28,2304]{3,1,2,0:T(8,128)}, f32[1,31,28,2304]{3,1,2,0:T(8,128)}) fusion(f32[1,32,28,2304]{3,1,2,0:T(8,128)S(1)} %get-tuple-element.376), kind=kLoop, calls=%fused_computation.225 | loop fusion | bytes 31997952 | tf_op jit(solution)/shard_map/vmap(jit(_roll_static))/slice | solution.py:16
  282.0 6.4 %fusion.99 = (f32[1,31,28,2304]{3,1,2,0:T(8,128)}, f32[1,31,28,2304]{3,1,2,0:T(8,128)}) fusion(f32[1,32,28,2304]{3,1,2,0:T(8,128)S(1)} %get-tuple-element.377), kind=kLoop, calls=%fused_computation.229 | loop fusion | bytes 31997952 | tf_op jit(solution)/shard_map/vmap(jit(_roll_static))/slice | solution.py:16
  289.6 20.4 %add_reduce_fusion = (f32[28,2304]{1,0:T(8,128)}, f32[28,2304]{1,0:T(8,128)}, f32[28,2304]{1,0:T(8,128)}) fusion(f32[1,32,28,2304]{3,1,2,0:T(8,128)S(1)} %get-tuple-element.377, f32[1,31,28,2304]{3,1,2,0:T(8,128)} %get-tuple-element.387, f32[1,1,28,2304]{3,1,2,0:T(1,128)} %get-tuple-element.389, f32[1,1,28,2304]{3,1,2,0:T(1,128)} %get-tuple-element.388, ...), kind=kLoop, calls=%fused_computation.111 | loop fusion | flops 67931136 | bytes 55738368 | tf_op jit(solution)/shard_map/vmap()/reduce_sum | solution.py:44
  322.9 34.2 %scatter_custom_fusion = s32[9216]{0:T(1024)S(1)} fusion(s32[9216]{0:T(1024)S(1)} %bitcast.309, s32[9216]{0:T(1024)S(1)} %iota.45, s32[]{:T(128)} %constant.186.clone.1), kind=kCustom, calls=%fused_computation.179 | custom fusion | bytes 36868 | tf_op jit(solution)/shard_map/scatter | solution.py:138
  360.8 33.4 %gather_fusion.1 = f32[9216,28]{1,0:T(8,128)} fusion(f32[28,9216]{0,1:T(8,128)} %bitcast.283, s32[9216]{0:T(1024)S(1)} %fusion.73), kind=kCustom, calls=%fused_computation.1 | custom fusion | bytes 2101248 | tf_op jit(solution)/shard_map/jit(_take)/gather | solution.py:140
  398.7 5.1 all-to-all-start.2
  405.4 31.7 %all-to-all-done.2 = f32[1,28,96,96]{3,2,0,1:T(8,128)S(1)} async-done(((f32[1,28,96,96]{3,2,0,1:T(8,128)}), f32[1,28,96,96]{3,2,0,1:T(8,128)S(1)}, u32[]{:S(2)}, u32[]{:S(2)}) %all-to-all-start.2) | async-done | bytes 1032224 | tf_op jit(solution)/shard_map/all_to_all | solution.py:143
  444.9 153.6 %while.19 = (s32[]{:T(128)}, f32[64,192]{1,0:T(8,128)S(1)}, f32[64,192]{1,0:T(8,128)S(1)}, f32[16,8,64,192]{3,2,1,0:T(8,128)}, s32[16,8]{0,1:T(8,128)S(1)}, /*in...) while((s32[]{:T(128)}, f32[64,192]{1,0:T(8,128)S(1)}, ...), condition=%wide.region_8.9_spmd.clone.clone, body=%wide.region_7.8_spmd.clone.clone.sunk | while | flops 926866 | bytes 3029748 | solution.py:85
  598.5 8.6 %copy.107 = f32[128,64,192]{0,2,1:T(8,128)} copy(f32[128,64,192]{2,1,0:T(8,128)} %bitcast.288) | data formatting | bytes 12582912 | tf_op jit(solution)/shard_map/reshape | solution.py:85
  608.6 7.7 %fusion.56 = f32[1,1,7,64,2,128]{5,2,4,3,1,0:T(8,128)S(1)} fusion(f32[7,192,2,64]{1,0,2,3:T(8,128)S(1)} %reshape.4408, f32[128,64,192]{0,2,1:T(8,128)} %copy.107, f32[192]{0:T(256)S(1)} %fusion.76), kind=kOutput, calls=%fused_computation.134 | convolution fusion | flops 265814016 | bytes 7439104 | tf_op jit(solution)/shard_map/leacs,nsa->lescn/dot_general | solution.py:151
  (371 shorter events, 142.4 us)
Async XLA Ops:
  0.6 8.1 %copy-start.11 = (s32[1,1,9216]{2,1,0:T(1,128)S(1)}, s32[1,1,9216]{2,1,0:T(1,128)}, u32[]{:S(2)}) copy-start(s32[1,1,9216]{2,1,0:T(1,128)} %param.10) | copy-start | bytes 110596
  141.3 2.6 copy-start.5
  143.9 58.0 %copy-start.3 = (f32[28,2304]{1,0:T(8,128)}, f32[28,2304]{1,0:T(8,128)S(1)}, u32[]{:S(2)}) copy-start(f32[28,2304]{1,0:T(8,128)S(1)} %get-tuple-element.423) | copy-start | bytes 774148
  143.9 7.5 %copy-start.8 = (f32[28,2304]{1,0:T(8,128)S(1)}, f32[28,2304]{1,0:T(8,128)}, u32[]{:S(2)}) copy-start(f32[28,2304]{1,0:T(8,128)} %broadcast_multiply_fusion.2) | copy-start | bytes 774148
  147.9 1.0 copy-start.9
  147.9 3.5 copy-start.2
  151.3 15.5 %copy-start.1 = (f32[1,31,28,2304]{3,1,2,0:T(8,128)}, f32[1,31,28,2304]{3,1,2,0:T(8,128)S(1)}, u32[]{:S(2)}) copy-start(f32[1,31,28,2304]{3,1,2,0:T(8,128)S(1)} %slice.206) | copy-start | bytes 23998468
  182.5 10.6 %copy-start = (f32[1,32,28,2304]{3,1,2,0:T(8,128)}, f32[1,32,28,2304]{3,1,2,0:T(8,128)S(1)}, u32[]{:S(2)}) copy-start(f32[1,32,28,2304]{3,1,2,0:T(8,128)S(1)} %get-tuple-element.336) | copy-start | bytes 24772612
  182.5 11.8 %slice-start.2 = ((s8[8257536]{0:T(1024)(128)(4,1)}), s8[4194304]{0:T(1024)(128)(4,1)S(1)}, s32[]{:S(2)}) async-start(s8[8257536]{0:T(1024)(128)(4,1)} %bitcast.281), calls=%async_computation.6 | async-start | bytes 8388608
  182.5 11.8 %slice-start.3 = ((s8[8257536]{0:T(1024)(128)(4,1)}), s8[4063232]{0:T(1024)(128)(4,1)S(1)}, s32[]{:S(2)}) async-start(s8[8257536]{0:T(1024)(128)(4,1)} %bitcast.281), calls=%async_computation.7 | async-start | bytes 8126464
  233.0 15.9 %slice-start = ((s8[8257536]{0:T(1024)(128)(4,1)}), s8[4194304]{0:T(1024)(128)(4,1)S(1)}, s32[]{:S(2)}) async-start(s8[8257536]{0:T(1024)(128)(4,1)} %bitcast.279), calls=%async_computation.4 | async-start | bytes 8388608
  233.0 15.9 %slice-start.1 = ((s8[8257536]{0:T(1024)(128)(4,1)}), s8[4063232]{0:T(1024)(128)(4,1)S(1)}, s32[]{:S(2)}) async-start(s8[8257536]{0:T(1024)(128)(4,1)} %bitcast.279), calls=%async_computation.5 | async-start | bytes 8126464
  282.0 7.6 %copy-start.4 = (f32[28,2304]{1,0:T(8,128)S(1)}, f32[28,2304]{1,0:T(8,128)}, u32[]{:S(2)}) copy-start(f32[28,2304]{1,0:T(8,128)} %copy-done.3) | copy-start | bytes 774148
  289.6 22.7 %copy-start.6 = (f32[1,4,28,2304]{3,1,2,0:T(4,128)S(1)}, f32[1,4,28,2304]{3,1,2,0:T(4,128)}, u32[]{:S(2)}) copy-start(f32[1,4,28,2304]{3,1,2,0:T(4,128)} %copy-done.5) | copy-start | bytes 3096580
  310.0 7.0 %copy-start.10 = (f32[28,2304]{1,0:T(8,128)S(1)}, f32[28,2304]{1,0:T(8,128)}, u32[]{:S(2)}) copy-start(f32[28,2304]{1,0:T(8,128)} %get-tuple-element.275) | copy-start | bytes 774148
  310.0 12.9 %copy-start.12 = (s32[1,1,9216]{2,1,0:T(1,128)S(1)}, s32[1,1,9216]{2,1,0:T(1,128)}, u32[]{:S(2)}) copy-start(s32[1,1,9216]{2,1,0:T(1,128)} %param.10) | copy-start | bytes 110596
  319.3 38.0 %all-to-all-start.1 = ((f32[8,1,32256]{2,1,0:T(1,128)}), f32[8,1,32256]{2,1,0:T(1,128)S(1)}, u32[]{:S(2)}, u32[]{:S(2)}) async-start(f32[8,1,32256]{2,1,0:T(1,128)} %reshape.4406), calls=%async_computation.1 | async-start | bytes 2064384 | tf_op jit(solution)/shard_map/all_to_all | solution.py:127
  360.8 36.6 %copy-start.7 = (f32[1,1,28,96,96]{4,3,2,1,0:T(8,128)S(1)}, f32[1,1,28,96,96]{4,3,2,1,0:T(8,128)}, u32[]{:S(2)}) copy-start(f32[1,1,28,96,96]{4,3,2,1,0:T(8,128)} %param.7) | copy-start | bytes 3096580
  394.2 9.7 %copy-start.13 = (s32[128]{0:T(128)S(1)}, s32[128]{0:T(128)}, u32[]{:S(2)}) copy-start(s32[128]{0:T(128)} %param.11) | copy-start | bytes 1540
  398.7 38.4 %all-to-all-start.2 = ((f32[1,28,96,96]{3,2,0,1:T(8,128)}), f32[1,28,96,96]{3,2,0,1:T(8,128)S(1)}, u32[]{:S(2)}, u32[]{:S(2)}) async-start(f32[1,28,96,96]{3,2,0,1:T(8,128)} %bitcast.25), calls=%async_computation.2 | async-start | bytes 2752512 | tf_op jit(solution)/shard_map/all_to_all | solution.py:143
  441.4 165.8 %all-to-all-start.3 = ((f32[7,1,96,2,128]{2,3,1,0,4:T(2,128)}), f32[7,1,96,2,128]{2,3,1,0,4:T(2,128)S(1)}, u32[]{:S(2)}, u32[]{:S(2)}) async-start(f32[7,1,96,2,128]{2,3,1,0,4:T(2,128)} %copy.109), calls=%async_computation.3 | async-start | bytes 1835008 | tf_op jit(solution)/shard_map/all_to_all | solution.py:153
where the time goes:
time: 625 us; the launch traced here: 618 us
  local copies, waits for them, and re-layouts  276 us (44%)
  other arithmetic  175 us (28%)
  loops' own time  81.3 us (13%)
  waiting for transfers between devices  31.7 us (5%)
  blocking collectives  30.3 us (5%)
  starting transfers between devices  12.2 us (2%)
  matrix products  9.01 us (1%)
    another operation x1, loops' own time, legendre_table(): lax.scan(march_forward, (empty, empty), jnp.arange(MMAX, dtype=jnp.int32)...  81.3 us
    gather x2, local copies, waits for them, and re-layouts, shards(): by_target = jnp.take(stacked, slot_table, axis=3).transpose(3, 0, 1, 2, 4)  74.6 us
    slice x15, local copies, waits for them, and re-layouts, transport(): forward = jnp.roll(values, -1, axis=0)  62.9 us
    reduce_sum x2, other arithmetic, cloud_model(): ground_precipitation = ground_precipitation + jnp.mean(condensed, axis=0)  46.8 us
    gather x2, local copies, waits for them, and re-layouts, shards(): column_tend = jnp.take(in_slot_order, inverse, axis=2)  36.6 us
    scatter x1, local copies, waits for them, and re-layouts, shards(): inverse = jnp.zeros((block_cols,), jnp.int32).at[slot_list].set(jnp.arang...  34.2 us
    all_to_all x1, waiting for transfers between devices, shards(): lax.all_to_all(fields_now, 'col', split_axis=1, concat_axis=3, tiled=True)  31.7 us
    all_to_all x1, blocking collectives, shards(): lax.all_to_all(outgoing, ('sec', 'lat'), split_axis=0, concat_axis=1, til...  30.3 us
  transfers between devices with their start and end apart: 3, of which 1 were waited for; matrix products, arithmetic and copies ran while one was open for 19% of the time, Pallas kernels for 0%

commit v1 on v0

--- a/solution.py
+++ b/solution.py
@@ -140,7 +140,9 @@
         column_tend = jnp.take(in_slot_order, inverse, axis=2)
     new_state = state + column_tend.reshape(members, 1, levels, band_rows, lon_block)
     fields_now = new_state[:, 0]
-    regrouped = lax.all_to_all(fields_now, "col", split_axis=1, concat_axis=3, tiled=True)
+    pieces = jnp.split(fields_now, lax.axis_size("col"), axis=1)
+    received = lax.all_to_all(jnp.stack(pieces), "col", 0, 0)
+    regrouped = jnp.concatenate(received, axis=3)
     trig_rows = trig_table(jnp.arange(NLON, dtype=jnp.int32), wave_table)
     spectra = jnp.einsum("elay,ycs->leacs", regrouped, trig_rows, precision=lax.Precision.HIGHEST)
     owner_count = MMAX // lat_bands

time: 625 us -> 602 us (0.963)
  other arithmetic: 175 us -> 147 us
    sqrt x32, other arithmetic: 20.6 us -> 0.77 us  [march_forward(): jnp.sqrt(numerator / bottom) * (cosine * current - retreat * previous)]
    sqrt x16, other arithmetic: 10.4 us -> 0.44 us  [march_forward(): jnp.sqrt(jnp.maximum(lower_deg * lower_deg - order_col * order_col, 0.0)...]
  transfers between devices with their start and end apart: 3 -> 3, of which waited for: 1 -> 1; matrix products, arithmetic and copies ran while one was open for 19% -> 15% of each run, Pallas kernels for 0% -> 0%
where the time goes in v1:
time: 602 us; the launch traced here: 595 us
  local copies, waits for them, and re-layouts  282 us (47%)
  other arithmetic  147 us (24%)
  loops' own time  80.2 us (13%)
  waiting for transfers between devices  32.3 us (5%)
  blocking collectives  30.3 us (5%)
  starting transfers between devices  12.3 us (2%)
  matrix products  10.2 us (2%)
    another operation x1, loops' own time, legendre_table(): lax.scan(march_forward, (empty, empty), jnp.arange(MMAX, dtype=jnp.int32)...  80.2 us
    gather x2, local copies, waits for them, and re-layouts, shards(): by_target = jnp.take(stacked, slot_table, axis=3).transpose(3, 0, 1, 2, 4)  74.6 us
    slice x15, local copies, waits for them, and re-layouts, transport(): forward = jnp.roll(values, -1, axis=0)  62.9 us
    reduce_sum x2, other arithmetic, cloud_model(): ground_precipitation = ground_precipitation + jnp.mean(condensed, axis=0)  46.8 us
    gather x2, local copies, waits for them, and re-layouts, shards(): column_tend = jnp.take(in_slot_order, inverse, axis=2)  37.5 us
    scatter x1, local copies, waits for them, and re-layouts, shards(): inverse = jnp.zeros((block_cols,), jnp.int32).at[slot_list].set(jnp.arang...  34.2 us
    all_to_all x1, waiting for transfers between devices, shards(): received = lax.all_to_all(jnp.stack(pieces), 'col', 0, 0)  32.3 us
    all_to_all x1, blocking collectives, shards(): lax.all_to_all(outgoing, ('sec', 'lat'), split_axis=0, concat_axis=1, til...  30.3 us
  transfers between devices with their start and end apart: 3, of which 1 were waited for; matrix products, arithmetic and copies ran while one was open for 15% of the time, Pallas kernels for 0%

profile of v1, /device:TPU:0, one launch (start us, length us, event | category | flops | bytes accessed | tf_op | source)
XLA Modules:
  0.0 595.5 jit_solution(8140534007367251549)
XLA Ops:
  8.8 12.9 %maximum_bitcast_fusion = f32[2,28,9216]{1,0,2:T(2,128)} fusion(f32[1,1,28,9216]{2,0,3,1:T(1,128)} %bitcast.290, f32[1,1,28,9216]{2,0,3,1:T(1,128)} %bitcast.289), kind=kLoop, calls=%fused_computation.84 | loop fusion | flops 516096 | bytes 4128768 | tf_op jit(solution)/shard_map/stack | solution.py:103
  21.7 66.6 %gather_fusion = f32[9216,2,28]{2,1,0:T(2,128)} fusion(f32[2,28,9216]{1,0,2:T(2,128)} %maximum_bitcast_fusion, s32[9216]{0:T(1024)S(1)} %broadcast_clamp_fusion), kind=kCustom, calls=%fused_computation | custom fusion | bytes 4165632 | tf_op jit(solution)/shard_map/jit(_take)/gather | solution.py:114
  88.3 8.0 %copy.118 = f32[8,1152,2,28]{1,0,2,3:T(8,128)S(1)} copy(f32[8,1152,2,28]{3,2,1,0:T(2,128)} %bitcast.291) | data formatting | bytes 4128768 | tf_op jit(solution)/shard_map/jit(_take)/gather | solution.py:114
  100.0 30.3 %all_to_all.38 = f32[8,1,64512]{2,1,0:T(1,128)S(1)} all-to-all(f32[8,1,64512]{2,1,0:T(1,128)S(1)} %copy.96), channel_id=1, replica_groups=mesh['sec'=4,'lat'=2,'col'=4] {'sec','lat'}, dimensions={0} | all-to-all | bytes 4128768 | tf_op jit(solution)/shard_map/all_to_all | solution.py:117
  130.3 6.9 %reduce.8 = f32[8,64512]{1,0:T(8,128)} reduce(f32[8,1,64512]{2,1,0:T(1,128)S(1)} %all_to_all.38, f32[]{:T(128)} %constant.239), dimensions={1}, to_apply=%all_to_all.12.reduce_sub_computation | reduce | bytes 4128772 | tf_op jit(solution)/shard_map/all_to_all | solution.py:117
  151.3 8.7 %fusion.44 = (f32[1,32,28,2304]{3,1,2,0:T(8,128)}, f32[1,32,28,2304]{3,1,2,0:T(8,128)S(1)}) fusion(f32[1,1,28,2304]{3,1,2,0:T(1,128)S(1)} %get-tuple-element.416, f32[1,31,28,2304]{3,1,2,0:T(8,128)S(1)} %slice.206, bf16[1,32,28,1,1,2304]{5,1,4,3,2,0:T(8,128)(2,1)S(1)} %copy-done.2, f32[28,2304]{1,0:T(8,128)S(1)} %get-tuple-element.422, ...), kind=kLoop, calls=%fused_computation.94 | loop fusion | flops 33030144 | bytes 30449664 | tf_op jit(solution)/shard_map/vmap()/add | solution.py:37
  160.1 6.4 %fusion.107 = (f32[1,31,28,2304]{3,1,2,0:T(8,128)}, f32[1,31,28,2304]{3,1,2,0:T(8,128)}) fusion(f32[1,32,28,2304]{3,1,2,0:T(8,128)S(1)} %get-tuple-element.407), kind=kLoop, calls=%fused_computation.241 | loop fusion | bytes 31997952 | tf_op jit(solution)/shard_map/vmap(jit(_roll_static))/slice | solution.py:16
  166.9 15.7 %fusion.51 = (f32[28,2304]{1,0:T(8,128)}, f32[28,2304]{1,0:T(8,128)}, f32[1,32,28,2304]{3,1,2,0:T(8,128)S(1)}) fusion(f32[28,2304]{1,0:T(8,128)S(1)} %get-tuple-element.422, bf16[1,32,28,1,1,2304]{5,1,4,3,2,0:T(8,128)(2,1)S(1)} %copy-done.2, f32[28,2304]{1,0:T(8,128)S(1)} %get-tuple-element.427, f32[28,2304]{1,0:T(8,128)S(1)} %copy-done.9, ...), kind=kLoop, calls=%fused_computation.125 | loop fusion | flops 67995648 | bytes 39481344 | tf_op jit(solution)/shard_map/vmap()/reduce_sum | solution.py:40
  182.6 8.4 %fusion.105 = (f32[1,31,28,2304]{3,1,2,0:T(8,128)}, f32[1,31,28,2304]{3,1,2,0:T(8,128)}) fusion(f32[1,32,28,2304]{3,1,2,0:T(8,128)S(1)} %get-tuple-element.336), kind=kLoop, calls=%fused_computation.239 | loop fusion | bytes 31997952 | tf_op jit(solution)/shard_map/vmap(jit(_roll_static))/slice | solution.py:16
  194.4 6.4 %fusion.103 = (f32[1,31,28,2304]{3,1,2,0:T(8,128)}, f32[1,31,28,2304]{3,1,2,0:T(8,128)}) fusion(f32[1,32,28,2304]{3,1,2,0:T(8,128)S(1)} %bitcast.287), kind=kLoop, calls=%fused_computation.237 | loop fusion | bytes 31997952 | tf_op jit(solution)/shard_map/vmap(jit(_roll_static))/slice | solution.py:16
  201.9 31.1 %fusion.52 = (f32[28,2304]{1,0:T(8,128)}, f32[1,32,28,2304]{3,1,2,0:T(8,128)}, f32[1,32,28,2304]{3,1,2,0:T(8,128)}) fusion(f32[28,2304]{1,0:T(8,128)S(1)} %get-tuple-element.423, f32[1,32,28,2304]{3,1,2,0:T(8,128)} %copy-done, f32[28,2304]{1,0:T(8,128)S(1)} %get-tuple-element.422, bf16[1,32,28,1,1,2304]{5,1,4,3,2,0:T(8,128)(2,1)S(1)} %copy-done.2, ...), kind=kLoop, calls=%fused_computation.126 | loop fusion | flops 96961536 | bytes 72253440 | tf_op jit(solution)/shard_map/vmap()/reduce_sum | solution.py:40
  233.0 12.5 %fusion.97 = (f32[1,31,28,2304]{3,1,2,0:T(8,128)}, f32[1,31,28,2304]{3,1,2,0:T(8,128)}) fusion(f32[1,32,28,2304]{3,1,2,0:T(8,128)} %get-tuple-element.338), kind=kLoop, calls=%fused_computation.231 | loop fusion | bytes 31997952 | tf_op jit(solution)/shard_map/vmap(jit(_roll_static))/slice | solution.py:16
  248.9 6.4 %fusion.101 = (f32[1,31,28,2304]{3,1,2,0:T(8,128)}, f32[1,31,28,2304]{3,1,2,0:T(8,128)}) fusion(f32[1,32,28,2304]{3,1,2,0:T(8,128)S(1)} %bitcast.285), kind=kLoop, calls=%fused_computation.235 | loop fusion | bytes 31997952 | tf_op jit(solution)/shard_map/vmap(jit(_roll_static))/slice | solution.py:16
  256.4 18.1 %subtract_add_fusion = (f32[1,32,28,2304]{3,1,2,0:T(8,128)S(1)}, f32[1,32,28,2304]{3,1,2,0:T(8,128)S(1)}) fusion(f32[1,32,28,2304]{3,1,2,0:T(8,128)} %get-tuple-element.338, f32[1,31,28,2304]{3,1,2,0:T(8,128)} %get-tuple-element.383, f32[1,1,28,2304]{3,1,2,0:T(1,128)} %get-tuple-element.385, f32[1,1,28,2304]{3,1,2,0:T(1,128)} %get-tuple-element.384, ...), kind=kLoop, calls=%fused_computation.114 | loop fusion | flops 55738368 | bytes 67092480 | tf_op jit(solution)/shard_map/vmap()/add | solution.py:39
  274.5 6.4 %fusion.95 = (f32[1,31,28,2304]{3,1,2,0:T(8,128)}, f32[1,31,28,2304]{3,1,2,0:T(8,128)}) fusion(f32[1,32,28,2304]{3,1,2,0:T(8,128)S(1)} %get-tuple-element.376), kind=kLoop, calls=%fused_computation.229 | loop fusion | bytes 31997952 | tf_op jit(solution)/shard_map/vmap(jit(_roll_static))/slice | solution.py:16
  282.0 6.4 %fusion.99 = (f32[1,31,28,2304]{3,1,2,0:T(8,128)}, f32[1,31,28,2304]{3,1,2,0:T(8,128)}) fusion(f32[1,32,28,2304]{3,1,2,0:T(8,128)S(1)} %get-tuple-element.377), kind=kLoop, calls=%fused_computation.233 | loop fusion | bytes 31997952 | tf_op jit(solution)/shard_map/vmap(jit(_roll_static))/slice | solution.py:16
  289.6 20.4 %add_reduce_fusion = (f32[28,2304]{1,0:T(8,128)}, f32[28,2304]{1,0:T(8,128)}, f32[28,2304]{1,0:T(8,128)}) fusion(f32[1,32,28,2304]{3,1,2,0:T(8,128)S(1)} %get-tuple-element.377, f32[1,31,28,2304]{3,1,2,0:T(8,128)} %get-tuple-element.387, f32[1,1,28,2304]{3,1,2,0:T(1,128)} %get-tuple-element.389, f32[1,1,28,2304]{3,1,2,0:T(1,128)} %get-tuple-element.388, ...), kind=kLoop, calls=%fused_computation.111 | loop fusion | flops 67931136 | bytes 55738368 | tf_op jit(solution)/shard_map/vmap()/reduce_sum | solution.py:44
  322.9 34.2 %scatter_custom_fusion = s32[9216]{0:T(1024)S(1)} fusion(s32[9216]{0:T(1024)S(1)} %bitcast.313, s32[9216]{0:T(1024)S(1)} %iota.45, s32[]{:T(128)} %constant.186.clone.1), kind=kCustom, calls=%fused_computation.183 | custom fusion | bytes 36868 | tf_op jit(solution)/shard_map/scatter | solution.py:138
  360.8 33.5 %gather_fusion.1 = f32[9216,28]{1,0:T(8,128)} fusion(f32[28,9216]{0,1:T(8,128)} %bitcast.288, s32[9216]{0:T(1024)S(1)} %fusion.73), kind=kCustom, calls=%fused_computation.1 | custom fusion | bytes 2101248 | tf_op jit(solution)/shard_map/jit(_take)/gather | solution.py:140
  401.3 5.1 all-to-all-start.2
  407.5 32.3 %all-to-all-done.2 = f32[4,1,7,96,96]{4,3,2,1,0:T(8,128)} async-done(((f32[4,1,7,96,96]{4,3,2,1,0:T(8,128)}), f32[4,1,7,96,96]{4,3,2,1,0:T(8,128)}, u32[]{:S(2)}, u32[]{:S(2)}) %all-to-all-start.2) | async-done | bytes 1032224 | tf_op jit(solution)/shard_map/all_to_all | solution.py:144
  453.5 122.8 %while.19 = (s32[]{:T(128)}, f32[64,192]{1,0:T(8,128)S(1)}, f32[64,192]{1,0:T(8,128)S(1)}, f32[16,8,64,192]{3,2,1,0:T(8,128)}, s32[16,8]{0,1:T(8,128)S(1)}, /*in...) while((s32[]{:T(128)}, f32[64,192]{1,0:T(8,128)S(1)}, ...), condition=%wide.region_8.9_spmd.clone.clone, body=%wide.region_7.8_spmd.clone.clone.sunk | while | flops 926866 | bytes 3029748 | solution.py:85
  576.2 8.6 %copy.107 = f32[128,64,192]{0,2,1:T(8,128)} copy(f32[128,64,192]{2,1,0:T(8,128)} %bitcast.293) | data formatting | bytes 12582912 | tf_op jit(solution)/shard_map/reshape | solution.py:85
  586.3 7.7 %fusion.56 = f32[1,1,7,64,2,128]{5,2,4,3,1,0:T(8,128)S(1)} fusion(f32[7,192,2,64]{1,0,2,3:T(8,128)S(1)} %reshape.4413, f32[128,64,192]{0,2,1:T(8,128)} %copy.107, f32[192]{0:T(256)S(1)} %fusion.76), kind=kOutput, calls=%fused_computation.134 | convolution fusion | flops 265814016 | bytes 7439104 | tf_op jit(solution)/shard_map/leacs,nsa->lescn/dot_general | solution.py:153
  (375 shorter events, 120.5 us)
Async XLA Ops:
  0.6 8.1 %copy-start.12 = (s32[1,1,9216]{2,1,0:T(1,128)S(1)}, s32[1,1,9216]{2,1,0:T(1,128)}, u32[]{:S(2)}) copy-start(s32[1,1,9216]{2,1,0:T(1,128)} %param.10) | copy-start | bytes 110596
  141.2 2.6 copy-start.5
  143.8 58.1 %copy-start.3 = (f32[28,2304]{1,0:T(8,128)}, f32[28,2304]{1,0:T(8,128)S(1)}, u32[]{:S(2)}) copy-start(f32[28,2304]{1,0:T(8,128)S(1)} %get-tuple-element.427) | copy-start | bytes 774148
  143.8 7.5 %copy-start.9 = (f32[28,2304]{1,0:T(8,128)S(1)}, f32[28,2304]{1,0:T(8,128)}, u32[]{:S(2)}) copy-start(f32[28,2304]{1,0:T(8,128)} %broadcast_multiply_fusion.2) | copy-start | bytes 774148
  147.8 1.0 copy-start.10
  147.8 3.5 copy-start.2
  151.3 15.6 %copy-start.1 = (f32[1,31,28,2304]{3,1,2,0:T(8,128)}, f32[1,31,28,2304]{3,1,2,0:T(8,128)S(1)}, u32[]{:S(2)}) copy-start(f32[1,31,28,2304]{3,1,2,0:T(8,128)S(1)} %slice.206) | copy-start | bytes 23998468
  182.6 10.6 %copy-start = (f32[1,32,28,2304]{3,1,2,0:T(8,128)}, f32[1,32,28,2304]{3,1,2,0:T(8,128)S(1)}, u32[]{:S(2)}) copy-start(f32[1,32,28,2304]{3,1,2,0:T(8,128)S(1)} %get-tuple-element.336) | copy-start | bytes 24772612
  182.6 11.8 %slice-start.2 = ((s8[8257536]{0:T(1024)(128)(4,1)}), s8[4194304]{0:T(1024)(128)(4,1)S(1)}, s32[]{:S(2)}) async-start(s8[8257536]{0:T(1024)(128)(4,1)} %bitcast.286), calls=%async_computation.6 | async-start | bytes 8388608
  182.6 11.8 %slice-start.3 = ((s8[8257536]{0:T(1024)(128)(4,1)}), s8[4063232]{0:T(1024)(128)(4,1)S(1)}, s32[]{:S(2)}) async-start(s8[8257536]{0:T(1024)(128)(4,1)} %bitcast.286), calls=%async_computation.7 | async-start | bytes 8126464
  233.0 15.8 %slice-start = ((s8[8257536]{0:T(1024)(128)(4,1)}), s8[4194304]{0:T(1024)(128)(4,1)S(1)}, s32[]{:S(2)}) async-start(s8[8257536]{0:T(1024)(128)(4,1)} %bitcast.284), calls=%async_computation.4 | async-start | bytes 8388608
  233.0 15.8 %slice-start.1 = ((s8[8257536]{0:T(1024)(128)(4,1)}), s8[4063232]{0:T(1024)(128)(4,1)S(1)}, s32[]{:S(2)}) async-start(s8[8257536]{0:T(1024)(128)(4,1)} %bitcast.284), calls=%async_computation.5 | async-start | bytes 8126464
  282.0 7.6 %copy-start.4 = (f32[28,2304]{1,0:T(8,128)S(1)}, f32[28,2304]{1,0:T(8,128)}, u32[]{:S(2)}) copy-start(f32[28,2304]{1,0:T(8,128)} %copy-done.3) | copy-start | bytes 774148
  289.6 22.7 %copy-start.6 = (f32[1,4,28,2304]{3,1,2,0:T(4,128)S(1)}, f32[1,4,28,2304]{3,1,2,0:T(4,128)}, u32[]{:S(2)}) copy-start(f32[1,4,28,2304]{3,1,2,0:T(4,128)} %copy-done.5) | copy-start | bytes 3096580
  310.0 7.0 %copy-start.11 = (f32[28,2304]{1,0:T(8,128)S(1)}, f32[28,2304]{1,0:T(8,128)}, u32[]{:S(2)}) copy-start(f32[28,2304]{1,0:T(8,128)} %get-tuple-element.275) | copy-start | bytes 774148
  310.0 12.9 %copy-start.13 = (s32[1,1,9216]{2,1,0:T(1,128)S(1)}, s32[1,1,9216]{2,1,0:T(1,128)}, u32[]{:S(2)}) copy-start(s32[1,1,9216]{2,1,0:T(1,128)} %param.10) | copy-start | bytes 110596
  319.3 38.0 %all-to-all-start.1 = ((f32[8,1,32256]{2,1,0:T(1,128)}), f32[8,1,32256]{2,1,0:T(1,128)S(1)}, u32[]{:S(2)}, u32[]{:S(2)}) async-start(f32[8,1,32256]{2,1,0:T(1,128)} %reshape.4411), calls=%async_computation.1 | async-start | bytes 2064384 | tf_op jit(solution)/shard_map/all_to_all | solution.py:127
  360.8 37.5 %copy-start.7 = (f32[1,1,28,96,96]{4,3,2,1,0:T(8,128)S(1)}, f32[1,1,28,96,96]{4,3,2,1,0:T(8,128)}, u32[]{:S(2)}) copy-start(f32[1,1,28,96,96]{4,3,2,1,0:T(8,128)} %param.7) | copy-start | bytes 3096580
  394.3 12.2 %copy-start.14 = (s32[128]{0:T(128)S(1)}, s32[128]{0:T(128)}, u32[]{:S(2)}) copy-start(s32[128]{0:T(128)} %param.11) | copy-start | bytes 1540
  399.8 50.1 %copy-start.8 = (f32[1,1,28,96,96]{4,3,2,1,0:T(8,128)}, f32[1,1,28,96,96]{4,3,2,1,0:T(8,128)S(1)}, u32[]{:S(2)}) copy-start(f32[1,1,28,96,96]{4,3,2,1,0:T(8,128)S(1)} %select_add_fusion) | copy-start | bytes 3096580
  401.3 38.5 %all-to-all-start.2 = ((f32[4,1,7,96,96]{4,3,2,1,0:T(8,128)}), f32[4,1,7,96,96]{4,3,2,1,0:T(8,128)}, u32[]{:S(2)}, u32[]{:S(2)}) async-start(f32[4,1,7,96,96]{4,3,2,1,0:T(8,128)} %pad_maximum_fusion.15), calls=%async_computation.2 | async-start | bytes 2752512 | tf_op jit(solution)/shard_map/all_to_all | solution.py:144
  449.9 135.0 %all-to-all-start.3 = ((f32[7,1,96,2,128]{2,3,1,0,4:T(2,128)}), f32[7,1,96,2,128]{2,3,1,0,4:T(2,128)S(1)}, u32[]{:S(2)}, u32[]{:S(2)}) async-start(f32[7,1,96,2,128]{2,3,1,0,4:T(2,128)} %copy.109), calls=%async_computation.3 | async-start | bytes 1835008 | tf_op jit(solution)/shard_map/all_to_all | solution.py:155
